TPU v7x, 32 devices: a whole 2x2x4 slice. The times are simulated.
32 devices in a mesh: dp: 8 (over z, x), fsdp: 4 (over y, core).
Axes of the slice: x: 2, y: 2, z: 4, core: 2. Of those that a mesh axis runs over, the one named last changes fastest.
Arguments:
- tokens: bfloat16 [2, 16, 1024, 768], P(None, 'dp', 'fsdp'), may hold values from -6 to 6
- cotangent: bfloat16 [2, 16, 1024, 768], P(None, 'dp', 'fsdp'), may hold values from -6 to 6
- lengths: int32 [2, 16], P(None, 'dp'), may hold values from 256 to 1024, as said below
- inward_weight: float32 [768, 2304], P('fsdp'), may hold values from -0.21875 to 0.21875
- outward_weight: float32 [768, 768], P('fsdp'), may hold values from -6 to 6
- expand_weight: float32 [768, 2304], P('fsdp'), may hold values from -0.21875 to 0.21875
- shrink_weight: float32 [1152, 768], P('fsdp'), may hold values from -0.1875 to 0.1875
- gain_weight: float32 [2, 768], P(None, 'fsdp'), may hold values from 0.5 to 1.5
- inward_first: float32 [768, 2304], P('fsdp'), may hold values from -2048 to 2048
- outward_first: float32 [768, 768], P('fsdp'), may hold values from -64 to 64
- expand_first: float32 [768, 2304], P('fsdp'), may hold values from -512 to 512
- shrink_first: float32 [1152, 768], P('fsdp'), may hold values from -512 to 512
- gain_first: float32 [2, 768], P(None, 'fsdp'), may hold values from -2048 to 2048
- inward_second: float32 [768, 2304], P('fsdp'), may hold values from 104857.6 to 419430.4
- outward_second: float32 [768, 768], P('fsdp'), may hold values from 131.072 to 524.288
- expand_second: float32 [768, 2304], P('fsdp'), may hold values from 6553.6 to 26214.4
- shrink_second: float32 [1152, 768], P('fsdp'), may hold values from 9502.72 to 38010.88
- gain_second: float32 [2, 768], P(None, 'fsdp'), may hold values from 104857.6 to 419430.4
Outputs:
- block_out: bfloat16 [2, 16, 1024, 768], P(None, 'dp', 'fsdp')
- input_grad: float32 [2, 16, 1024, 768], P(None, 'dp', 'fsdp')
- inward_renewed: float32 [768, 2304], P('fsdp')
- inward_momentum: float32 [768, 2304], P('fsdp')
- inward_variance: float32 [768, 2304], P('fsdp')
- outward_renewed: float32 [768, 768], P('fsdp')
- outward_momentum: float32 [768, 768], P('fsdp')
- outward_variance: float32 [768, 768], P('fsdp')
- expand_renewed: float32 [768, 2304], P('fsdp')
- expand_momentum: float32 [768, 2304], P('fsdp')
- expand_variance: float32 [768, 2304], P('fsdp')
- shrink_renewed: float32 [1152, 768], P('fsdp')
- shrink_momentum: float32 [1152, 768], P('fsdp')
- shrink_variance: float32 [1152, 768], P('fsdp')
- gain_renewed: float32 [2, 768], P(None, 'fsdp')
- gain_momentum: float32 [2, 768], P(None, 'fsdp')
- gain_variance: float32 [2, 768], P(None, 'fsdp')
Inputs may be any that keep to these rules, and one draw needn't show every extreme that they name: `lengths`: in each micro-batch, among the 2 sequences of each dp index, one has length 1024.
All inputs are finite; a program needn't handle non-finite values.
Results may differ from a plain program's by a relative error of at most 0.014.
Values may be sent and summed in bfloat16 or wider, within the bound.
No kernel may reach another device: no remote copies, remote signals or barrier semaphores. Data moves between devices by JAX's collectives and lax.ppermute only.
A program may use at most 256 MiB of HBM per device.

v0:
```python
import jax
import jax.numpy as jnp
from jax import lax
from jax.sharding import PartitionSpec as P

FF = 1152
HEADS = 12
HDIM = 64
STEP = 10
rope_base = 160000.0
norm_eps = 1e-05
adam_beta = 0.5
adam_eps = 1e-08
weight_decay = 0.01
rates = (0.07, 2.0, 0.07, 0.06, 0.2)
masked_score = -1e30


def tables(positions):
    half_dim = HDIM // 2
    exponent = jnp.arange(half_dim, dtype=jnp.float32) * (2.0 / HDIM)
    inverse = jnp.power(jnp.float32(rope_base), -exponent)
    angles = positions.astype(jnp.float32)[:, None] * inverse[None, :]
    return (jnp.cos(angles), jnp.sin(angles))


def rotate(values, cosine, sine_table):
    half_dim = values.shape[-1] // 2
    former = values[..., :half_dim]
    latter = values[..., half_dim:]
    cos_wide = cosine[:, None, :]
    sin_wide = sine_table[:, None, :]
    return jnp.concatenate(
        [former * cos_wide - latter * sin_wide, latter * cos_wide + former * sin_wide], axis=-1
    )


def normalize(values, gain_row):
    center = values - jnp.mean(values, axis=-1, keepdims=True)
    spread = jnp.mean(center * center, axis=-1, keepdims=True)
    return center * lax.rsqrt(spread + norm_eps) * gain_row


def geglu(joined_heads):
    gate_part = joined_heads[..., :FF]
    upward = joined_heads[..., FF:]
    return 0.5 * gate_part * (1.0 + lax.erf(gate_part * 0.7071067811865476)) * upward


def attention_scores(queries, keys_all, live_keys, score_scale):
    product = (
        jnp.einsum("sqhd,skhd->shqk", queries, keys_all, preferred_element_type=jnp.float32)
        * score_scale
    )
    return jnp.where(live_keys[:, None, None, :], product, masked_score)


def adam_update(master, gradient, moment_one, moment_two, step_rate, decay_rate):
    first_new = adam_beta * moment_one + (1.0 - adam_beta) * gradient
    second_new = adam_beta * moment_two + (1.0 - adam_beta) * gradient * gradient
    correction = 1.0 - adam_beta**STEP
    direction = first_new / correction / (jnp.sqrt(second_new / correction) + adam_eps)
    renewed = master - step_rate * (direction + decay_rate * master)
    return (renewed, first_new, second_new)


def local(
    tokens,
    cotangent,
    lengths,
    inward_weight,
    outward_weight,
    expand_weight,
    shrink_weight,
    gain_weight,
    inward_first,
    outward_first,
    expand_first,
    shrink_first,
    gain_first,
    inward_second,
    outward_second,
    expand_second,
    shrink_second,
    gain_second,
):
    micro_count, group_size, local_len, model_width = tokens.shape
    seq_total = local_len * lax.axis_size("fsdp")
    row_count = group_size * local_len
    score_scale = HDIM ** (-0.5)
    positions = lax.axis_index("fsdp") * local_len + jnp.arange(local_len, dtype=jnp.int32)
    cosine, sine_table = tables(positions)
    key_positions = jnp.arange(seq_total, dtype=jnp.int32)
    inward_copy = inward_weight.astype(jnp.bfloat16)
    outward_copy = outward_weight.astype(jnp.bfloat16)
    expand_copy = expand_weight.astype(jnp.bfloat16)
    shrink_copy = shrink_weight.astype(jnp.bfloat16)
    gain_copy = gain_weight.astype(jnp.bfloat16)
    accum = (
        jnp.zeros((model_width, 3 * model_width), jnp.float32),
        jnp.zeros((model_width, model_width), jnp.float32),
        jnp.zeros((model_width, 2 * FF), jnp.float32),
        jnp.zeros((FF, model_width), jnp.float32),
        jnp.zeros((2, model_width), jnp.float32),
    )

    def micro_step(accum, item):
        input_tokens, incoming, limits = item
        gathered = (
            lax.all_gather(inward_copy, "fsdp", axis=0, tiled=True),
            lax.all_gather(outward_copy, "fsdp", axis=0, tiled=True),
            lax.all_gather(expand_copy, "fsdp", axis=0, tiled=True),
            lax.all_gather(shrink_copy, "fsdp", axis=0, tiled=True),
            lax.all_gather(gain_copy, "fsdp", axis=1, tiled=True),
        )
        inward_matrix, outward_matrix, expand_matrix, shrink_matrix, gain_full = gathered
        gain_rows = gain_full.astype(jnp.float32)
        live_keys = key_positions[None, :] < limits[:, None]
        live_rows = (positions[None, :] < limits[:, None]).astype(jnp.float32).reshape(row_count, 1)
        flat_in = input_tokens.astype(jnp.float32).reshape(row_count, model_width)
        hidden_first_norm = normalize(flat_in, gain_rows[0]).astype(jnp.bfloat16)
        joined_heads = jnp.dot(
            hidden_first_norm, inward_matrix, preferred_element_type=jnp.float32
        ).reshape(group_size, local_len, 3, HEADS, HDIM)
        queries = rotate(joined_heads[:, :, 0], cosine, sine_table).astype(jnp.bfloat16)
        keys_local = rotate(joined_heads[:, :, 1], cosine, sine_table).astype(jnp.bfloat16)
        values_local = joined_heads[:, :, 2].astype(jnp.bfloat16)
        keys_all, values_all = (
            lax.all_gather(keys_local, "fsdp", axis=1, tiled=True),
            lax.all_gather(values_local, "fsdp", axis=1, tiled=True),
        )
        scores = attention_scores(queries, keys_all, live_keys, score_scale)
        row_peak = jnp.max(scores, axis=-1, keepdims=True)
        exp_terms = jnp.exp(scores - row_peak)
        totals = jnp.sum(exp_terms, axis=-1, keepdims=True)
        attention_low = (exp_terms / totals).astype(jnp.bfloat16)
        log_total = row_peak + jnp.log(totals)
        mixed_tokens = jnp.einsum(
            "shqk,skhd->sqhd", attention_low, values_all, preferred_element_type=jnp.float32
        )
        mixed_tokens = mixed_tokens.astype(jnp.bfloat16).reshape(row_count, model_width)
        middle_state = flat_in + jnp.dot(
            mixed_tokens, outward_matrix, preferred_element_type=jnp.float32
        )
        hidden_second_norm = normalize(middle_state, gain_rows[1]).astype(jnp.bfloat16)
        expanded_rows = jnp.dot(
            hidden_second_norm, expand_matrix, preferred_element_type=jnp.float32
        )
        hidden_state = geglu(expanded_rows).astype(jnp.bfloat16)
        layer_result = (
            middle_state + jnp.dot(hidden_state, shrink_matrix, preferred_element_type=jnp.float32)
        ) * live_rows
        block_rows = layer_result.astype(jnp.bfloat16).reshape(group_size, local_len, model_width)
        gathered_back = (
            lax.all_gather(inward_copy, "fsdp", axis=0, tiled=True),
            lax.all_gather(outward_copy, "fsdp", axis=0, tiled=True),
            lax.all_gather(expand_copy, "fsdp", axis=0, tiled=True),
            lax.all_gather(shrink_copy, "fsdp", axis=0, tiled=True),
            lax.all_gather(gain_copy, "fsdp", axis=1, tiled=True),
        )
        inward_back, outward_back, expand_back, shrink_back, gain_back = gathered_back
        gain_rows_back = gain_back.astype(jnp.float32)
        grad_out = incoming.astype(jnp.float32).reshape(row_count, model_width) * live_rows
        branch_low = grad_out.astype(jnp.bfloat16)
        shrink_grad = jnp.einsum(
            "rf,rd->fd", hidden_state, branch_low, preferred_element_type=jnp.float32
        )
        hidden_grad = jnp.einsum(
            "rd,fd->rf", branch_low, shrink_back, preferred_element_type=jnp.float32
        )
        unused, geglu_back = jax.vjp(geglu, expanded_rows)
        expanded_grad = geglu_back(hidden_grad)[0].astype(jnp.bfloat16)
        expand_grad = jnp.einsum(
            "rd,re->de", hidden_second_norm, expanded_grad, preferred_element_type=jnp.float32
        )
        h_two_grad = jnp.einsum(
            "re,de->rd", expanded_grad, expand_back, preferred_element_type=jnp.float32
        )
        unused, second_back = jax.vjp(normalize, middle_state, gain_rows_back[1])
        middle_part, gain_two_grad = second_back(h_two_grad)
        middle_grad = grad_out + middle_part
        mixer_low = middle_grad.astype(jnp.bfloat16)
        outward_grad = jnp.einsum(
            "rd,re->de", mixed_tokens, mixer_low, preferred_element_type=jnp.float32
        )
        mixed_grad = jnp.einsum(
            "re,de->rd", mixer_low, outward_back, preferred_element_type=jnp.float32
        )
        mixed_grad = mixed_grad.astype(jnp.bfloat16).reshape(group_size, local_len, HEADS, HDIM)
        scores_again = attention_scores(queries, keys_all, live_keys, score_scale)
        attention = jnp.exp(scores_again - log_total)
        attention_again = attention.astype(jnp.bfloat16)
        attention_grad = jnp.einsum(
            "sqhd,skhd->shqk", mixed_grad, values_all, preferred_element_type=jnp.float32
        )
        row_inner = jnp.sum(attention * attention_grad, axis=-1, keepdims=True)
        score_grad = (attention * (attention_grad - row_inner)).astype(jnp.bfloat16)
        query_grad = (
            jnp.einsum("shqk,skhd->sqhd", score_grad, keys_all, preferred_element_type=jnp.float32)
            * score_scale
        )
        key_part = (
            jnp.einsum("shqk,sqhd->skhd", score_grad, queries, preferred_element_type=jnp.float32)
            * score_scale
        )
        value_part = jnp.einsum(
            "shqk,sqhd->skhd", attention_again, mixed_grad, preferred_element_type=jnp.float32
        )
        key_grad, value_grad = (
            lax.psum_scatter(
                key_part.astype(jnp.bfloat16), "fsdp", scatter_dimension=1, tiled=True
            ).astype(jnp.float32),
            lax.psum_scatter(
                value_part.astype(jnp.bfloat16), "fsdp", scatter_dimension=1, tiled=True
            ).astype(jnp.float32),
        )
        joined_grad = jnp.stack(
            [
                rotate(query_grad, cosine, -sine_table),
                rotate(key_grad, cosine, -sine_table),
                value_grad,
            ],
            axis=2,
        )
        joined_grad = joined_grad.reshape(row_count, 3 * model_width).astype(jnp.bfloat16)
        inward_grad = jnp.einsum(
            "rd,re->de", hidden_first_norm, joined_grad, preferred_element_type=jnp.float32
        )
        h_one_grad = jnp.einsum(
            "re,de->rd", joined_grad, inward_back, preferred_element_type=jnp.float32
        )
        unused, first_back = jax.vjp(normalize, flat_in, gain_rows_back[0])
        input_part, gain_one_grad = first_back(h_one_grad)
        input_rows = (middle_grad + input_part).reshape(group_size, local_len, model_width)
        gain_grad = jnp.stack([gain_one_grad, gain_two_grad])
        accum = jax.tree.map(
            jnp.add, accum, (inward_grad, outward_grad, expand_grad, shrink_grad, gain_grad)
        )
        return (accum, (block_rows, input_rows))

    accum, outputs = lax.scan(micro_step, accum, (tokens, cotangent, lengths))
    block_out, input_grad = outputs
    shards = (
        lax.psum_scatter(
            accum[0].astype(jnp.bfloat16), "fsdp", scatter_dimension=0, tiled=True
        ).astype(jnp.float32),
        lax.psum_scatter(
            accum[1].astype(jnp.bfloat16), "fsdp", scatter_dimension=0, tiled=True
        ).astype(jnp.float32),
        lax.psum_scatter(
            accum[2].astype(jnp.bfloat16), "fsdp", scatter_dimension=0, tiled=True
        ).astype(jnp.float32),
        lax.psum_scatter(
            accum[3].astype(jnp.bfloat16), "fsdp", scatter_dimension=0, tiled=True
        ).astype(jnp.float32),
        lax.psum_scatter(
            accum[4].astype(jnp.bfloat16), "fsdp", scatter_dimension=1, tiled=True
        ).astype(jnp.float32),
    )
    shards = lax.psum((shards[0], shards[1], shards[2], shards[3], shards[4]), "dp")
    inward_new = adam_update(
        inward_weight, shards[0], inward_first, inward_second, rates[0], weight_decay
    )
    outward_new = adam_update(
        outward_weight, shards[1], outward_first, outward_second, rates[1], weight_decay
    )
    expand_new = adam_update(
        expand_weight, shards[2], expand_first, expand_second, rates[2], weight_decay
    )
    shrink_new = adam_update(
        shrink_weight, shards[3], shrink_first, shrink_second, rates[3], weight_decay
    )
    gain_new = adam_update(gain_weight, shards[4], gain_first, gain_second, rates[4], 0.0)
    return (
        block_out,
        input_grad,
        inward_new[0],
        inward_new[1],
        inward_new[2],
        outward_new[0],
        outward_new[1],
        outward_new[2],
        expand_new[0],
        expand_new[1],
        expand_new[2],
        shrink_new[0],
        shrink_new[1],
        shrink_new[2],
        gain_new[0],
        gain_new[1],
        gain_new[2],
    )


def solution(mesh):
    in_specs = (
        P(None, "dp", "fsdp", None),
        P(None, "dp", "fsdp", None),
        P(None, "dp"),
        P("fsdp", None),
        P("fsdp", None),
        P("fsdp", None),
        P("fsdp", None),
        P(None, "fsdp"),
        P("fsdp", None),
        P("fsdp", None),
        P("fsdp", None),
        P("fsdp", None),
        P(None, "fsdp"),
        P("fsdp", None),
        P("fsdp", None),
        P("fsdp", None),
        P("fsdp", None),
        P(None, "fsdp"),
    )
    out_specs = (
        P(None, "dp", "fsdp", None),
        P(None, "dp", "fsdp", None),
        P("fsdp", None),
        P("fsdp", None),
        P("fsdp", None),
        P("fsdp", None),
        P("fsdp", None),
        P("fsdp", None),
        P("fsdp", None),
        P("fsdp", None),
        P("fsdp", None),
        P("fsdp", None),
        P("fsdp", None),
        P("fsdp", None),
        P(None, "fsdp"),
        P(None, "fsdp"),
        P(None, "fsdp"),
    )
    return jax.shard_map(local, mesh=mesh, in_specs=in_specs, out_specs=out_specs, check_vma=False)
```

profile of v0, /device:TPU:0, one launch (start us, length us, event | category | flops | bytes accessed | tf_op | source)
XLA Modules:
  0.0 1104.0 jit_solution(12216921466018292153)
XLA Ops:
  14.0 698.6 %while.26 = (s32[]{:T(128)}, f32[768,2304]{1,0:T(8,128)}, f32[768,768]{1,0:T(8,128)}, f32[768,2304]{1,0:T(8,128)}, f32[1152,768]{1,0:T(8,128)}, /*index=5*/f32[2...) while((s32[]{:T(128)}, f32[768,2304]{1,0:T(8,128)}, ...), condition=%wide.region_16.17_spmd.clone.clone.clone, body=%wide.region_0.16_spmd.clone.clone.clone.sunk | while | flops 20481859584 | bytes 894956672 | solution.py:241
  23.4 27.1 %all-gather.19.cloned.1.call-done = bf16[768,2304]{1,0:T(8,128)(2,1)} async-done(((bf16[192,2304]{1,0:T(8,128)(2,1)}), bf16[768,2304]{1,0:T(8,128)(2,1)}) %all-gather.19.cloned.1.call-update) | async-done | bytes 3538960 | tf_op jit(solution)/shard_map/while/body/eval_jaxpr/all_gather | solution.py:110
  73.4 19.9 %all-gather.21.cloned.1.call-done = bf16[2,1024,12,64]{1,3,2,0:T(8,128)(2,1)} async-done(((bf16[2,256,12,64]{1,3,2,0:T(8,128)(2,1)}), bf16[2,1024,12,64]{1,3,2,0:T(8,128)(2,1)}) %all-gather.21.cloned.1.call-update) | async-done | bytes 3145744 | tf_op jit(solution)/shard_map/while/body/eval_jaxpr/all_gather | solution.py:129
  93.3 12.8 %fusion.184 = (f32[2,12,256]{2,1,0:T(8,128)S(1)}, f32[2,12,256,1024]{3,2,1,0:T(8,128)}) fusion(pred[2,1024]{1,0:T(4,128)(4,1)S(1)} %iota_compare_fusion.2, bf16[2,1024,12,64]{1,3,2,0:T(8,128)(2,1)} %all-gather.21.cloned.1.call-done, bf16[2,256,12,32]{1,3,2,0:T(8,128)(2,1)S(1)} %get-tuple-element.666, bf16[2,256,12,32]{1,3,2,0:T(8,128)(2,1)S(1)} %get-tuple-element.667), kind=kOutput, calls=%fused_computation.16.clone.1 | convolution fusion | flops 825747456 | bytes 29124608 | tf_op jit(solution)/shard_map/while/body/eval_jaxpr/sqhd,skhd->shqk/dot_general | solution.py:52
  148.6 28.0 %all-gather.27.cloned.1.call-done = bf16[768,2304]{1,0:T(8,128)(2,1)} async-done(((bf16[192,2304]{1,0:T(8,128)(2,1)}), bf16[768,2304]{1,0:T(8,128)(2,1)}) %all-gather.27.cloned.1.call-update) | async-done | bytes 3538960 | tf_op jit(solution)/shard_map/while/body/eval_jaxpr/all_gather | solution.py:112
  183.0 16.4 %all-gather.29.cloned.1.call-done = bf16[1152,768]{1,0:T(8,128)(2,1)} async-done(((bf16[288,768]{1,0:T(8,128)(2,1)}), bf16[1152,768]{1,0:T(8,128)(2,1)}) %all-gather.29.cloned.1.call-update) | async-done | bytes 1769488 | tf_op jit(solution)/shard_map/while/body/eval_jaxpr/all_gather | solution.py:158
  218.7 19.6 %multiply_reduce_fusion.9 = (f32[2,12,256]{2,1,0:T(8,128)}, f32[2,12,256,1024]{3,2,1,0:T(8,128)}) fusion(f32[2,12,256]{2,1,0:T(8,128)} %log_add_fusion.2, f32[2,12,256,1024]{3,2,1,0:T(8,128)} %get-tuple-element.669, pred[2,1024]{1,0:T(4,128)(4,1)S(1)} %iota_compare_fusion.2, bf16[2,1024,1,12,64]{1,4,3,2,0:T(8,128)(2,1)} %all-gather.23.cloned.1.call-done, ...), kind=kOutput, calls=%fused_computation.6.clone.1 | convolution fusion | flops 836757504 | bytes 54315008 | tf_op jit(solution)/shard_map/while/body/eval_jaxpr/sqhd,skhd->shqk/dot_general | solution.py:193
  238.2 16.9 %multiply_convert_fusion.13 = bf16[2,12,256,1024]{3,2,1,0:T(8,128)(2,1)S(1)} fusion(f32[2,12,256,1024]{3,2,1,0:T(8,128)} %get-tuple-element.681, f32[2,12,256]{2,1,0:T(8,128)} %get-tuple-element.682, f32[2,12,256]{2,1,0:T(8,128)} %log_add_fusion.2, f32[2,12,256,1024]{3,2,1,0:T(8,128)} %get-tuple-element.669, pred[2,1024]{1,0:T(4,128)(4,1)S(1)} %iota_compare_fusion.2), kind=kLoop, calls=%fused_computation.5.clone.1 | loop fusion | flops 37748736 | bytes 62965760 | tf_op jit(solution)/shard_map/while/body/eval_jaxpr/convert_element_type | solution.py:197
  264.4 14.4 %convert_bitcast_fusion.2 = bf16[2,1024,12,64]{1,3,2,0:T(8,128)(2,1)} fusion(f32[2,12,256]{2,1,0:T(8,128)S(1)} %copy-done.37, f32[2,12,256,1024]{3,2,1,0:T(8,128)} %get-tuple-element.669, pred[2,1024]{1,0:T(4,128)(4,1)S(1)} %iota_compare_fusion.2, bf16[2,256,12,64]{1,0,3,2:T(2,128)(2,1)} %reshape.379), kind=kOutput, calls=%fused_computation.27.clone.1 | convolution fusion | flops 832045056 | bytes 29124608 | tf_op jit(solution)/shard_map/while/body/eval_jaxpr/shqk,sqhd->skhd/dot_general | solution.py:206
  309.2 33.2 %reduce-scatter.20.cloned.1.call-done = bf16[2,256,12,64]{1,3,2,0:T(8,128)(2,1)} async-done(((bf16[2,1024,12,64]{1,3,2,0:T(8,128)(2,1)}), bf16[2,256,12,64]{1,3,2,0:T(8,128)(2,1)}) %reduce-scatter.20.cloned.1.call-update) | async-done | bytes 786448 | tf_op jit(solution)/shard_map/while/body/eval_jaxpr/reduce_scatter | solution.py:213
  370.6 25.4 %all-gather.19.cloned.1.call-done = bf16[768,2304]{1,0:T(8,128)(2,1)} async-done(((bf16[192,2304]{1,0:T(8,128)(2,1)}), bf16[768,2304]{1,0:T(8,128)(2,1)}) %all-gather.19.cloned.1.call-update) | async-done | bytes 3538960 | tf_op jit(solution)/shard_map/while/body/eval_jaxpr/all_gather | solution.py:110
  419.1 19.6 %all-gather.21.cloned.1.call-done = bf16[2,1024,12,64]{1,3,2,0:T(8,128)(2,1)} async-done(((bf16[2,256,12,64]{1,3,2,0:T(8,128)(2,1)}), bf16[2,1024,12,64]{1,3,2,0:T(8,128)(2,1)}) %all-gather.21.cloned.1.call-update) | async-done | bytes 3145744 | tf_op jit(solution)/shard_map/while/body/eval_jaxpr/all_gather | solution.py:129
  438.8 12.8 %fusion.184 = (f32[2,12,256]{2,1,0:T(8,128)S(1)}, f32[2,12,256,1024]{3,2,1,0:T(8,128)}) fusion(pred[2,1024]{1,0:T(4,128)(4,1)S(1)} %iota_compare_fusion.2, bf16[2,1024,12,64]{1,3,2,0:T(8,128)(2,1)} %all-gather.21.cloned.1.call-done, bf16[2,256,12,32]{1,3,2,0:T(8,128)(2,1)S(1)} %get-tuple-element.666, bf16[2,256,12,32]{1,3,2,0:T(8,128)(2,1)S(1)} %get-tuple-element.667), kind=kOutput, calls=%fused_computation.16.clone.1 | convolution fusion | flops 825747456 | bytes 29124608 | tf_op jit(solution)/shard_map/while/body/eval_jaxpr/sqhd,skhd->shqk/dot_general | solution.py:52
  494.1 28.2 %all-gather.27.cloned.1.call-done = bf16[768,2304]{1,0:T(8,128)(2,1)} async-done(((bf16[192,2304]{1,0:T(8,128)(2,1)}), bf16[768,2304]{1,0:T(8,128)(2,1)}) %all-gather.27.cloned.1.call-update) | async-done | bytes 3538960 | tf_op jit(solution)/shard_map/while/body/eval_jaxpr/all_gather | solution.py:112
  528.7 16.4 %all-gather.29.cloned.1.call-done = bf16[1152,768]{1,0:T(8,128)(2,1)} async-done(((bf16[288,768]{1,0:T(8,128)(2,1)}), bf16[1152,768]{1,0:T(8,128)(2,1)}) %all-gather.29.cloned.1.call-update) | async-done | bytes 1769488 | tf_op jit(solution)/shard_map/while/body/eval_jaxpr/all_gather | solution.py:158
  564.3 19.8 %multiply_reduce_fusion.9 = (f32[2,12,256]{2,1,0:T(8,128)}, f32[2,12,256,1024]{3,2,1,0:T(8,128)}) fusion(f32[2,12,256]{2,1,0:T(8,128)} %log_add_fusion.2, f32[2,12,256,1024]{3,2,1,0:T(8,128)} %get-tuple-element.669, pred[2,1024]{1,0:T(4,128)(4,1)S(1)} %iota_compare_fusion.2, bf16[2,1024,1,12,64]{1,4,3,2,0:T(8,128)(2,1)} %all-gather.23.cloned.1.call-done, ...), kind=kOutput, calls=%fused_computation.6.clone.1 | convolution fusion | flops 836757504 | bytes 54315008 | tf_op jit(solution)/shard_map/while/body/eval_jaxpr/sqhd,skhd->shqk/dot_general | solution.py:193
  584.1 16.9 %multiply_convert_fusion.13 = bf16[2,12,256,1024]{3,2,1,0:T(8,128)(2,1)S(1)} fusion(f32[2,12,256,1024]{3,2,1,0:T(8,128)} %get-tuple-element.681, f32[2,12,256]{2,1,0:T(8,128)} %get-tuple-element.682, f32[2,12,256]{2,1,0:T(8,128)} %log_add_fusion.2, f32[2,12,256,1024]{3,2,1,0:T(8,128)} %get-tuple-element.669, pred[2,1024]{1,0:T(4,128)(4,1)S(1)} %iota_compare_fusion.2), kind=kLoop, calls=%fused_computation.5.clone.1 | loop fusion | flops 37748736 | bytes 62965760 | tf_op jit(solution)/shard_map/while/body/eval_jaxpr/convert_element_type | solution.py:197
  610.3 14.3 %convert_bitcast_fusion.2 = bf16[2,1024,12,64]{1,3,2,0:T(8,128)(2,1)} fusion(f32[2,12,256]{2,1,0:T(8,128)S(1)} %copy-done.37, f32[2,12,256,1024]{3,2,1,0:T(8,128)} %get-tuple-element.669, pred[2,1024]{1,0:T(4,128)(4,1)S(1)} %iota_compare_fusion.2, bf16[2,256,12,64]{1,0,3,2:T(2,128)(2,1)} %reshape.379), kind=kOutput, calls=%fused_computation.27.clone.1 | convolution fusion | flops 832045056 | bytes 29124608 | tf_op jit(solution)/shard_map/while/body/eval_jaxpr/shqk,sqhd->skhd/dot_general | solution.py:206
  658.1 30.1 %reduce-scatter.20.cloned.1.call-done = bf16[2,256,12,64]{1,3,2,0:T(8,128)(2,1)} async-done(((bf16[2,1024,12,64]{1,3,2,0:T(8,128)(2,1)}), bf16[2,256,12,64]{1,3,2,0:T(8,128)(2,1)}) %reduce-scatter.20.cloned.1.call-update) | async-done | bytes 786448 | tf_op jit(solution)/shard_map/while/body/eval_jaxpr/reduce_scatter | solution.py:213
  736.6 27.8 %reduce-scatter.12.cloned.1.call-done = bf16[192,768]{1,0:T(8,128)(2,1)} async-done(((bf16[768,768]{1,0:T(8,128)(2,1)}), bf16[192,768]{1,0:T(8,128)(2,1)}) %reduce-scatter.12.cloned.1.call-update) | async-done | bytes 294928 | tf_op jit(solution)/shard_map/reduce_scatter | solution.py:247
  764.4 32.5 %reduce-scatter.16.cloned.1.call-done = bf16[288,768]{1,0:T(8,128)(2,1)} async-done(((bf16[1152,768]{1,0:T(8,128)(2,1)}), bf16[288,768]{1,0:T(8,128)(2,1)}) %reduce-scatter.16.cloned.1.call-update) | async-done | bytes 442384 | tf_op jit(solution)/shard_map/reduce_scatter | solution.py:253
  797.0 42.9 %reduce-scatter.10.cloned.1.call-done = bf16[192,2304]{1,0:T(8,128)(2,1)} async-done(((bf16[768,2304]{1,0:T(8,128)(2,1)}), bf16[192,2304]{1,0:T(8,128)(2,1)}) %reduce-scatter.10.cloned.1.call-update) | async-done | bytes 884752 | tf_op jit(solution)/shard_map/reduce_scatter | solution.py:244
  839.9 43.1 %reduce-scatter.14.cloned.1.call-done = bf16[192,2304]{1,0:T(8,128)(2,1)} async-done(((bf16[768,2304]{1,0:T(8,128)(2,1)}), bf16[192,2304]{1,0:T(8,128)(2,1)}) %reduce-scatter.14.cloned.1.call-update) | async-done | bytes 884752 | tf_op jit(solution)/shard_map/reduce_scatter | solution.py:250
  882.9 199.7 %all-reduce.4 = (f32[192,2304]{1,0:T(8,128)}, f32[192,768]{1,0:T(8,128)}, f32[192,2304]{1,0:T(8,128)}, f32[288,768]{1,0:T(8,128)}, f32[2,192]{1,0:T(2,128)S(1)}) all-reduce(bf16[192,2304]{1,0:T(8,128)(2,1)} %reduce-scatter.10.cloned.1.call-done, ...), channel_id=1, replica_groups=mesh['dp'=8,'fsdp'=4] {'dp'}, use_global_device_ids=true, to_apply=%region_18.19 | all-reduce | flops 1253760 | bytes 7522560 | tf_op jit(solution)/shard_map/psum | solution.py:260
  (506 shorter events, 363.3 us)
Async XLA Ops:
  14.0 36.5 %all-gather.19.cloned.1.call-start = ((), (), s32[]{:S(2)}) async-start(), calls=%async_computation.12 | async-start | bytes 4423680 | tf_op jit(solution)/shard_map/while/body/eval_jaxpr/all_gather | solution.py:110
  14.9 78.4 %all-gather.21.cloned.1.call-start = ((), (), s32[]{:S(2)}) async-start(), calls=%async_computation.13 | async-start | bytes 3932160 | tf_op jit(solution)/shard_map/while/body/eval_jaxpr/all_gather | solution.py:129
  64.2 60.2 %all-gather.23.cloned.1.call-start = ((), (), s32[]{:S(2)}) async-start(), calls=%async_computation.14 | async-start | bytes 3932160 | tf_op jit(solution)/shard_map/while/body/eval_jaxpr/all_gather | solution.py:130
  66.6 77.3 %all-gather.25.cloned.1.call-start = ((), (), s32[]{:S(2)}) async-start(), calls=%async_computation.15 | async-start | bytes 1474560 | tf_op jit(solution)/shard_map/while/body/eval_jaxpr/all_gather | solution.py:111
  67.2 109.5 %all-gather.27.cloned.1.call-start = ((), (), s32[]{:S(2)}) async-start(), calls=%async_computation.16 | async-start | bytes 4423680 | tf_op jit(solution)/shard_map/while/body/eval_jaxpr/all_gather | solution.py:112
  67.8 131.7 %all-gather.29.cloned.1.call-start = ((), (), s32[]{:S(2)}) async-start(), calls=%async_computation.17 | async-start | bytes 2211840 | tf_op jit(solution)/shard_map/while/body/eval_jaxpr/all_gather | solution.py:158
  68.4 238.9 %reduce-scatter.22.cloned.1.call-start = ((), (), s32[]{:S(2)}) async-start(), calls=%async_computation.19 | async-start | bytes 3932160 | tf_op jit(solution)/shard_map/while/body/eval_jaxpr/reduce_scatter | solution.py:210
  263.7 78.8 %reduce-scatter.20.cloned.1.call-start = ((), (), s32[]{:S(2)}) async-start(), calls=%async_computation.18 | async-start | bytes 3932160 | tf_op jit(solution)/shard_map/while/body/eval_jaxpr/reduce_scatter | solution.py:213
  362.2 33.8 %all-gather.19.cloned.1.call-start = ((), (), s32[]{:S(2)}) async-start(), calls=%async_computation.12 | async-start | bytes 4423680 | tf_op jit(solution)/shard_map/while/body/eval_jaxpr/all_gather | solution.py:110
  363.1 75.7 %all-gather.21.cloned.1.call-start = ((), (), s32[]{:S(2)}) async-start(), calls=%async_computation.13 | async-start | bytes 3932160 | tf_op jit(solution)/shard_map/while/body/eval_jaxpr/all_gather | solution.py:129
  409.7 60.2 %all-gather.23.cloned.1.call-start = ((), (), s32[]{:S(2)}) async-start(), calls=%async_computation.14 | async-start | bytes 3932160 | tf_op jit(solution)/shard_map/while/body/eval_jaxpr/all_gather | solution.py:130
  412.2 77.2 %all-gather.25.cloned.1.call-start = ((), (), s32[]{:S(2)}) async-start(), calls=%async_computation.15 | async-start | bytes 1474560 | tf_op jit(solution)/shard_map/while/body/eval_jaxpr/all_gather | solution.py:111
  412.7 109.6 %all-gather.27.cloned.1.call-start = ((), (), s32[]{:S(2)}) async-start(), calls=%async_computation.16 | async-start | bytes 4423680 | tf_op jit(solution)/shard_map/while/body/eval_jaxpr/all_gather | solution.py:112
  413.5 131.6 %all-gather.29.cloned.1.call-start = ((), (), s32[]{:S(2)}) async-start(), calls=%async_computation.17 | async-start | bytes 2211840 | tf_op jit(solution)/shard_map/while/body/eval_jaxpr/all_gather | solution.py:158
  414.1 242.1 %reduce-scatter.22.cloned.1.call-start = ((), (), s32[]{:S(2)}) async-start(), calls=%async_computation.19 | async-start | bytes 3932160 | tf_op jit(solution)/shard_map/while/body/eval_jaxpr/reduce_scatter | solution.py:210
  609.6 78.6 %reduce-scatter.20.cloned.1.call-start = ((), (), s32[]{:S(2)}) async-start(), calls=%async_computation.18 | async-start | bytes 3932160 | tf_op jit(solution)/shard_map/while/body/eval_jaxpr/reduce_scatter | solution.py:213
  712.5 23.2 %reduce-scatter.18.cloned.1.call-start = ((), (), s32[]{:S(2)}) async-start(), calls=%async_computation.11 | async-start | bytes 245760
  714.2 50.3 %reduce-scatter.12.cloned.1.call-start = ((), (), s32[]{:S(2)}) async-start(), calls=%async_computation.8 | async-start | bytes 1474560 | tf_op jit(solution)/shard_map/reduce_scatter | solution.py:247
  717.2 79.8 %reduce-scatter.16.cloned.1.call-start = ((), (), s32[]{:S(2)}) async-start(), calls=%async_computation.10 | async-start | bytes 2211840 | tf_op jit(solution)/shard_map/reduce_scatter | solution.py:253
  718.7 121.2 %reduce-scatter.10.cloned.1.call-start = ((), (), s32[]{:S(2)}) async-start(), calls=%async_computation.7 | async-start | bytes 4423680 | tf_op jit(solution)/shard_map/reduce_scatter | solution.py:244
  723.9 159.0 %reduce-scatter.14.cloned.1.call-start = ((), (), s32[]{:S(2)}) async-start(), calls=%async_computation.9 | async-start | bytes 4423680 | tf_op jit(solution)/shard_map/reduce_scatter | solution.py:250
  729.1 357.2 %copy-start.52 = (f32[288,768]{1,0:T(8,128)S(1)}, f32[288,768]{1,0:T(8,128)}, u32[]{:S(2)}) copy-start(f32[288,768]{1,0:T(8,128)} %param.31) | copy-start | bytes 2654212
  729.1 353.5 %copy-start.70 = (f32[2,192]{1,0:T(2,128)S(1)}, f32[2,192]{1,0:T(2,128)}, u32[]{:S(2)}) copy-start(f32[2,192]{1,0:T(2,128)} %param.27) | copy-start | bytes 4612
  729.1 354.1 %copy-start.45 = (f32[192,768]{1,0:T(8,128)S(1)}, f32[192,768]{1,0:T(8,128)}, u32[]{:S(2)}) copy-start(f32[192,768]{1,0:T(8,128)} %param.24) | copy-start | bytes 1769476
  (143 other events, 1759.3 us)
Sparse Core Ops, SparseCore 0:
  17.0 33.4 all-gather.18
  64.3 28.9 all-gather.20
  95.4 28.9 all-gather.22
  126.4 17.4 all-gather.24
  145.9 30.7 all-gather.26
  178.7 20.7 all-gather.28
  263.8 37.9 reduce-scatter.21
  304.5 37.9 reduce-scatter.19
  365.2 30.7 all-gather.18
  409.8 28.9 all-gather.20
  440.9 28.9 all-gather.22
  471.9 17.4 all-gather.24
  491.5 30.7 all-gather.26
  524.3 20.7 all-gather.28
  609.7 37.9 reduce-scatter.21
  650.3 37.9 reduce-scatter.19
Sparse Core Ops, SparseCore 1:
  716.0 19.7 reduce-scatter.17
  738.8 25.6 reduce-scatter.11
  767.7 29.3 reduce-scatter.15
  799.6 40.2 reduce-scatter.9
  842.6 40.2 reduce-scatter.13
where the time goes:
time: 1110 us; the launch traced here: 1100 us
  waiting for transfers between devices  424 us (38%)
  matrix products  233 us (21%)
  blocking collectives  211 us (19%)
  other arithmetic  118 us (11%)
  local copies, waits for them, and re-layouts  94.6 us (9%)
  between operations  15.9 us (1%)
    psum x1, blocking collectives, local(): lax.psum((shards[0], shards[1], shards[2], shards[3], shards[4]), 'dp')  200 us
    reduce_scatter x2, waiting for transfers between devices, micro_step(): lax.psum_scatter(value_part.astype(jnp.bfloat16), 'fsdp', scatter_dimensi...  63.3 us
    all_gather x2, waiting for transfers between devices, micro_step(): lax.all_gather(expand_copy, 'fsdp', axis=0, tiled=True)  56.2 us
    all_gather x2, waiting for transfers between devices, micro_step(): lax.all_gather(inward_copy, 'fsdp', axis=0, tiled=True)  52.4 us
    while x270, local copies, waits for them, and re-layouts  51.2 us
    reduce_scatter x1, waiting for transfers between devices, local(): lax.psum_scatter(accum[2].astype(jnp.bfloat16), 'fsdp', scatter_dimension...  43.1 us
    reduce_scatter x1, waiting for transfers between devices, local(): lax.psum_scatter(accum[0].astype(jnp.bfloat16), 'fsdp', scatter_dimension...  42.9 us
    all_gather x2, waiting for transfers between devices, micro_step(): lax.all_gather(keys_local, 'fsdp', axis=1, tiled=True)  39.5 us
  transfers between devices with their start and end apart: 21, of which 19 were waited for; matrix products, arithmetic and copies ran while one was open for 19% of the time, Pallas kernels for 0%

commit v1 on v0

--- a/solution.py
+++ b/solution.py
@@ -14,6 +14,28 @@
 weight_decay = 0.01
 rates = (0.07, 2.0, 0.07, 0.06, 0.2)
 masked_score = -1e30
+
+
+def laid_out(blocks, dim):
+    blocks = jnp.moveaxis(blocks, 0, dim)
+    shape = blocks.shape
+    return blocks.reshape(*shape[:dim], shape[dim] * shape[dim + 1], *shape[dim + 2 :])
+
+
+def collect(x, axis, dim):
+    size = lax.axis_size(axis)
+    pairs = [(i, (i + 1) % size) for i in range(size)]
+    back = [(b, a) for a, b in pairs]
+    lower, upper = ([], [])
+    for step in range(size - 1):
+        if step % 2 == 0:
+            lower.append(lax.ppermute(lower[-1] if lower else x, axis, pairs))
+        else:
+            upper.append(lax.ppermute(upper[-1] if upper else x, axis, back))
+    pieces = jnp.stack([*lower[::-1], x, *upper])
+    shift = lax.axis_index(axis) - len(lower)
+    pieces = pieces[(jnp.arange(size) - shift) % size]
+    return laid_out(pieces, dim)
 
 
 def tables(positions):
@@ -126,7 +148,7 @@
         keys_local = rotate(joined_heads[:, :, 1], cosine, sine_table).astype(jnp.bfloat16)
         values_local = joined_heads[:, :, 2].astype(jnp.bfloat16)
         keys_all, values_all = (
-            lax.all_gather(keys_local, "fsdp", axis=1, tiled=True),
+            collect(keys_local, "fsdp", 1),
             lax.all_gather(values_local, "fsdp", axis=1, tiled=True),
         )
         scores = attention_scores(queries, keys_all, live_keys, score_scale)

time: 1110 us -> 1070 us (0.964)
  waiting for transfers between devices: 424 us -> 369 us
    ppermute x0 -> x6, waiting for transfers between devices: none -> 80.9 us  [the longest x4 80.9 us: collect(): lower.append(lax.ppermute(lower[-1] if lower else x, axis, pairs))]
    all_gather x2, waiting for transfers between devices: 56.2 us -> 0.01 us  [micro_step(): lax.all_gather(expand_copy, 'fsdp', axis=0, tiled=True)]
    all_gather x2 -> x0, waiting for transfers between devices: 39.5 us -> none  [micro_step(): lax.all_gather(keys_local, 'fsdp', axis=1, tiled=True)]
    all_gather x2, waiting for transfers between devices: 13.7 us -> 0.01 us  [micro_step(): lax.all_gather(values_local, 'fsdp', axis=1, tiled=True)]
    while x270 -> x286, local copies, waits for them, and re-layouts: 51.2 us -> 49 us
  transfers between devices with their start and end apart: 21 -> 25, of which waited for: 19 -> 15; matrix products, arithmetic and copies ran while one was open for 19% -> 22% of each run, Pallas kernels for 0% -> 0%
where the time goes in v1:
time: 1070 us
  waiting for transfers between devices  369 us (34%)
  matrix products  236 us (22%)
  blocking collectives  211 us (20%)
  other arithmetic  126 us (12%)
  local copies, waits for them, and re-layouts  101 us (9%)
  between operations  15.8 us (1%)
    psum x1, blocking collectives, local(): lax.psum((shards[0], shards[1], shards[2], shards[3], shards[4]), 'dp')  200 us
    ppermute x4, waiting for transfers between devices, collect(): lower.append(lax.ppermute(lower[-1] if lower else x, axis, pairs))  80.9 us
    reduce_scatter x2, waiting for transfers between devices, micro_step(): lax.psum_scatter(value_part.astype(jnp.bfloat16), 'fsdp', scatter_dimensi...  59.4 us
    all_gather x2, waiting for transfers between devices, micro_step(): lax.all_gather(inward_copy, 'fsdp', axis=0, tiled=True)  52.4 us
    while x286, local copies, waits for them, and re-layouts  49 us
    reduce_scatter x1, waiting for transfers between devices, local(): lax.psum_scatter(accum[2].astype(jnp.bfloat16), 'fsdp', scatter_dimension...  43.1 us
    reduce_scatter x1, waiting for transfers between devices, local(): lax.psum_scatter(accum[0].astype(jnp.bfloat16), 'fsdp', scatter_dimension...  42.9 us
    dot_general x2, matrix products, micro_step(): jnp.einsum('sqhd,skhd->shqk', mixed_grad, values_all, preferred_element_t...  39.3 us
  transfers between devices with their start and end apart: 25, of which 15 were waited for; matrix products, arithmetic and copies ran while one was open for 22% of the time, Pallas kernels for 0%

profile of v1, /device:TPU:0, one launch (start us, length us, event | category | flops | bytes accessed | tf_op | source)
XLA Modules:
  0.0 1070.3 jit_solution(12357917258198014570)
XLA Ops:
  14.6 664.4 %while.27 = (s32[]{:T(128)}, f32[768,2304]{1,0:T(8,128)}, f32[768,768]{1,0:T(8,128)}, f32[768,2304]{1,0:T(8,128)}, f32[1152,768]{1,0:T(8,128)}, /*index=5*/f32[2...) while((s32[]{:T(128)}, f32[768,2304]{1,0:T(8,128)}, ...), condition=%wide.region_16.17_spmd.clone.clone.clone, body=%wide.region_0.16_spmd.clone.clone.clone.sunk | while | flops 20497588224 | bytes 911273408 | solution.py:263
  24.0 27.0 %all-gather.18.cloned.1.call-done = bf16[768,2304]{1,0:T(8,128)(2,1)} async-done(((bf16[192,2304]{1,0:T(8,128)(2,1)}), bf16[768,2304]{1,0:T(8,128)(2,1)}) %all-gather.18.cloned.1.call-update) | async-done | bytes 3538960 | tf_op jit(solution)/shard_map/while/body/eval_jaxpr/all_gather | solution.py:132
  72.3 32.6 %collective-permute-done.1 = bf16[2,256,12,64]{1,3,2,0:T(8,128)(2,1)S(1)} collective-permute-done((bf16[2,256,12,64]{1,3,2,0:T(8,128)(2,1)}, bf16[2,256,12,64]{1,3,2,0:T(8,128)(2,1)S(1)}, u32[]{:S(2)}, u32[]{:S(2)}) %collective-permute-start.1) | collective-permute-done | bytes 786464 | tf_op jit(solution)/shard_map/while/body/eval_jaxpr/ppermute | solution.py:32
  132.8 12.0 %fusion.189 = f32[2,12,256]{2,1,0:T(8,128)S(1)} fusion(f32[2,12,256]{2,1,0:T(8,128)S(1)} %get-tuple-element.734, f32[2,12,256,1024]{3,2,1,0:T(8,128)} %get-tuple-element.735, pred[2,1024]{1,0:T(4,128)(4,1)S(1)} %iota_compare_fusion.2), kind=kLoop, calls=%fused_computation.12.clone.1 | loop fusion | flops 25159680 | bytes 25217024 | tf_op jit(solution)/shard_map/while/body/eval_jaxpr/reduce_sum | solution.py:157
  146.1 12.8 %fusion.190 = bf16[2,256,12,64]{1,3,2,0:T(8,128)(2,1)S(1)} fusion(f32[2,12,256]{2,1,0:T(8,128)} %copy-done.48, f32[2,12,256]{2,1,0:T(8,128)} %copy-done.41, f32[2,12,256,1024]{3,2,1,0:T(8,128)} %get-tuple-element.735, pred[2,1024]{1,0:T(4,128)(4,1)S(1)} %iota_compare_fusion.2, bf16[2,1024,1,12,64]{1,4,3,2,0:T(8,128)(2,1)} %all-gather.20.cloned.1.call-done), kind=kOutput, calls=%fused_computation.71.clone.1 | convolution fusion | flops 837156864 | bytes 29149184 | tf_op jit(solution)/shard_map/while/body/eval_jaxpr/shqk,skhd->sqhd/dot_general | solution.py:160
  172.8 11.1 %all-gather.26.cloned.1.call-done = bf16[1152,768]{1,0:T(8,128)(2,1)} async-done(((bf16[288,768]{1,0:T(8,128)(2,1)}), bf16[1152,768]{1,0:T(8,128)(2,1)}) %all-gather.26.cloned.1.call-update) | async-done | bytes 1769488 | tf_op jit(solution)/shard_map/while/body/eval_jaxpr/all_gather | solution.py:180
  203.1 19.5 %multiply_reduce_fusion.9 = (f32[2,12,256]{2,1,0:T(8,128)}, f32[2,12,256,1024]{3,2,1,0:T(8,128)}) fusion(f32[2,12,256]{2,1,0:T(8,128)} %log_add_fusion.2, f32[2,12,256,1024]{3,2,1,0:T(8,128)} %get-tuple-element.735, pred[2,1024]{1,0:T(4,128)(4,1)S(1)} %iota_compare_fusion.2, bf16[2,1024,1,12,64]{1,4,3,2,0:T(8,128)(2,1)} %all-gather.20.cloned.1.call-done, ...), kind=kOutput, calls=%fused_computation.7.clone.1 | convolution fusion | flops 836757504 | bytes 54315008 | tf_op jit(solution)/shard_map/while/body/eval_jaxpr/sqhd,skhd->shqk/dot_general | solution.py:215
  222.6 16.9 %multiply_convert_fusion.13 = bf16[2,12,256,1024]{3,2,1,0:T(8,128)(2,1)S(1)} fusion(f32[2,12,256,1024]{3,2,1,0:T(8,128)} %get-tuple-element.747, f32[2,12,256]{2,1,0:T(8,128)} %get-tuple-element.748, f32[2,12,256]{2,1,0:T(8,128)} %log_add_fusion.2, f32[2,12,256,1024]{3,2,1,0:T(8,128)} %get-tuple-element.735, pred[2,1024]{1,0:T(4,128)(4,1)S(1)} %iota_compare_fusion.2), kind=kLoop, calls=%fused_computation.6.clone.1 | loop fusion | flops 37748736 | bytes 62965760 | tf_op jit(solution)/shard_map/while/body/eval_jaxpr/convert_element_type | solution.py:219
  248.8 14.4 %convert_bitcast_fusion.2 = bf16[2,1024,12,64]{1,3,2,0:T(8,128)(2,1)} fusion(f32[2,12,256]{2,1,0:T(8,128)S(1)} %copy-done.42, f32[2,12,256,1024]{3,2,1,0:T(8,128)} %get-tuple-element.735, pred[2,1024]{1,0:T(4,128)(4,1)S(1)} %iota_compare_fusion.2, bf16[2,256,12,64]{1,0,3,2:T(2,128)(2,1)} %reshape.524), kind=kOutput, calls=%fused_computation.29.clone.1 | convolution fusion | flops 832045056 | bytes 29124608 | tf_op jit(solution)/shard_map/while/body/eval_jaxpr/shqk,sqhd->skhd/dot_general | solution.py:228
  295.1 31.9 %reduce-scatter.20.cloned.1.call-done = bf16[2,256,12,64]{1,3,2,0:T(8,128)(2,1)} async-done(((bf16[2,1024,12,64]{1,3,2,0:T(8,128)(2,1)}), bf16[2,256,12,64]{1,3,2,0:T(8,128)(2,1)}) %reduce-scatter.20.cloned.1.call-update) | async-done | bytes 786448 | tf_op jit(solution)/shard_map/while/body/eval_jaxpr/reduce_scatter | solution.py:235
  354.1 25.4 %all-gather.18.cloned.1.call-done = bf16[768,2304]{1,0:T(8,128)(2,1)} async-done(((bf16[192,2304]{1,0:T(8,128)(2,1)}), bf16[768,2304]{1,0:T(8,128)(2,1)}) %all-gather.18.cloned.1.call-update) | async-done | bytes 3538960 | tf_op jit(solution)/shard_map/while/body/eval_jaxpr/all_gather | solution.py:132
  400.7 32.7 %collective-permute-done.1 = bf16[2,256,12,64]{1,3,2,0:T(8,128)(2,1)S(1)} collective-permute-done((bf16[2,256,12,64]{1,3,2,0:T(8,128)(2,1)}, bf16[2,256,12,64]{1,3,2,0:T(8,128)(2,1)S(1)}, u32[]{:S(2)}, u32[]{:S(2)}) %collective-permute-start.1) | collective-permute-done | bytes 786464 | tf_op jit(solution)/shard_map/while/body/eval_jaxpr/ppermute | solution.py:32
  461.2 12.0 %fusion.189 = f32[2,12,256]{2,1,0:T(8,128)S(1)} fusion(f32[2,12,256]{2,1,0:T(8,128)S(1)} %get-tuple-element.734, f32[2,12,256,1024]{3,2,1,0:T(8,128)} %get-tuple-element.735, pred[2,1024]{1,0:T(4,128)(4,1)S(1)} %iota_compare_fusion.2), kind=kLoop, calls=%fused_computation.12.clone.1 | loop fusion | flops 25159680 | bytes 25217024 | tf_op jit(solution)/shard_map/while/body/eval_jaxpr/reduce_sum | solution.py:157
  474.5 12.6 %fusion.190 = bf16[2,256,12,64]{1,3,2,0:T(8,128)(2,1)S(1)} fusion(f32[2,12,256]{2,1,0:T(8,128)} %copy-done.48, f32[2,12,256]{2,1,0:T(8,128)} %copy-done.41, f32[2,12,256,1024]{3,2,1,0:T(8,128)} %get-tuple-element.735, pred[2,1024]{1,0:T(4,128)(4,1)S(1)} %iota_compare_fusion.2, bf16[2,1024,1,12,64]{1,4,3,2,0:T(8,128)(2,1)} %all-gather.20.cloned.1.call-done), kind=kOutput, calls=%fused_computation.71.clone.1 | convolution fusion | flops 837156864 | bytes 29149184 | tf_op jit(solution)/shard_map/while/body/eval_jaxpr/shqk,skhd->sqhd/dot_general | solution.py:160
  501.0 11.2 %all-gather.26.cloned.1.call-done = bf16[1152,768]{1,0:T(8,128)(2,1)} async-done(((bf16[288,768]{1,0:T(8,128)(2,1)}), bf16[1152,768]{1,0:T(8,128)(2,1)}) %all-gather.26.cloned.1.call-update) | async-done | bytes 1769488 | tf_op jit(solution)/shard_map/while/body/eval_jaxpr/all_gather | solution.py:180
  531.5 19.7 %multiply_reduce_fusion.9 = (f32[2,12,256]{2,1,0:T(8,128)}, f32[2,12,256,1024]{3,2,1,0:T(8,128)}) fusion(f32[2,12,256]{2,1,0:T(8,128)} %log_add_fusion.2, f32[2,12,256,1024]{3,2,1,0:T(8,128)} %get-tuple-element.735, pred[2,1024]{1,0:T(4,128)(4,1)S(1)} %iota_compare_fusion.2, bf16[2,1024,1,12,64]{1,4,3,2,0:T(8,128)(2,1)} %all-gather.20.cloned.1.call-done, ...), kind=kOutput, calls=%fused_computation.7.clone.1 | convolution fusion | flops 836757504 | bytes 54315008 | tf_op jit(solution)/shard_map/while/body/eval_jaxpr/sqhd,skhd->shqk/dot_general | solution.py:215
  551.3 16.9 %multiply_convert_fusion.13 = bf16[2,12,256,1024]{3,2,1,0:T(8,128)(2,1)S(1)} fusion(f32[2,12,256,1024]{3,2,1,0:T(8,128)} %get-tuple-element.747, f32[2,12,256]{2,1,0:T(8,128)} %get-tuple-element.748, f32[2,12,256]{2,1,0:T(8,128)} %log_add_fusion.2, f32[2,12,256,1024]{3,2,1,0:T(8,128)} %get-tuple-element.735, pred[2,1024]{1,0:T(4,128)(4,1)S(1)} %iota_compare_fusion.2), kind=kLoop, calls=%fused_computation.6.clone.1 | loop fusion | flops 37748736 | bytes 62965760 | tf_op jit(solution)/shard_map/while/body/eval_jaxpr/convert_element_type | solution.py:219
  577.5 14.3 %convert_bitcast_fusion.2 = bf16[2,1024,12,64]{1,3,2,0:T(8,128)(2,1)} fusion(f32[2,12,256]{2,1,0:T(8,128)S(1)} %copy-done.42, f32[2,12,256,1024]{3,2,1,0:T(8,128)} %get-tuple-element.735, pred[2,1024]{1,0:T(4,128)(4,1)S(1)} %iota_compare_fusion.2, bf16[2,256,12,64]{1,0,3,2:T(2,128)(2,1)} %reshape.524), kind=kOutput, calls=%fused_computation.29.clone.1 | convolution fusion | flops 832045056 | bytes 29124608 | tf_op jit(solution)/shard_map/while/body/eval_jaxpr/shqk,sqhd->skhd/dot_general | solution.py:228
  627.9 27.5 %reduce-scatter.20.cloned.1.call-done = bf16[2,256,12,64]{1,3,2,0:T(8,128)(2,1)} async-done(((bf16[2,1024,12,64]{1,3,2,0:T(8,128)(2,1)}), bf16[2,256,12,64]{1,3,2,0:T(8,128)(2,1)}) %reduce-scatter.20.cloned.1.call-update) | async-done | bytes 786448 | tf_op jit(solution)/shard_map/while/body/eval_jaxpr/reduce_scatter | solution.py:235
  703.0 27.8 %reduce-scatter.12.cloned.1.call-done = bf16[192,768]{1,0:T(8,128)(2,1)} async-done(((bf16[768,768]{1,0:T(8,128)(2,1)}), bf16[192,768]{1,0:T(8,128)(2,1)}) %reduce-scatter.12.cloned.1.call-update) | async-done | bytes 294928 | tf_op jit(solution)/shard_map/reduce_scatter | solution.py:269
  730.8 32.5 %reduce-scatter.16.cloned.1.call-done = bf16[288,768]{1,0:T(8,128)(2,1)} async-done(((bf16[1152,768]{1,0:T(8,128)(2,1)}), bf16[288,768]{1,0:T(8,128)(2,1)}) %reduce-scatter.16.cloned.1.call-update) | async-done | bytes 442384 | tf_op jit(solution)/shard_map/reduce_scatter | solution.py:275
  763.3 42.9 %reduce-scatter.10.cloned.1.call-done = bf16[192,2304]{1,0:T(8,128)(2,1)} async-done(((bf16[768,2304]{1,0:T(8,128)(2,1)}), bf16[192,2304]{1,0:T(8,128)(2,1)}) %reduce-scatter.10.cloned.1.call-update) | async-done | bytes 884752 | tf_op jit(solution)/shard_map/reduce_scatter | solution.py:266
  806.3 43.1 %reduce-scatter.14.cloned.1.call-done = bf16[192,2304]{1,0:T(8,128)(2,1)} async-done(((bf16[768,2304]{1,0:T(8,128)(2,1)}), bf16[192,2304]{1,0:T(8,128)(2,1)}) %reduce-scatter.14.cloned.1.call-update) | async-done | bytes 884752 | tf_op jit(solution)/shard_map/reduce_scatter | solution.py:272
  849.3 199.6 %all-reduce.4 = (f32[192,2304]{1,0:T(8,128)}, f32[192,768]{1,0:T(8,128)}, f32[192,2304]{1,0:T(8,128)}, f32[288,768]{1,0:T(8,128)}, f32[2,192]{1,0:T(2,128)S(1)}) all-reduce(bf16[192,2304]{1,0:T(8,128)(2,1)} %reduce-scatter.10.cloned.1.call-done, ...), channel_id=1, replica_groups=mesh['dp'=8,'fsdp'=4] {'dp'}, use_global_device_ids=true, to_apply=%region_18.19 | all-reduce | flops 1253760 | bytes 7522560 | tf_op jit(solution)/shard_map/psum | solution.py:282
  (536 shorter events, 350.9 us)
Async XLA Ops:
  14.6 36.5 %all-gather.18.cloned.1.call-start = ((), (), s32[]{:S(2)}) async-start(), calls=%async_computation.12 | async-start | bytes 4423680 | tf_op jit(solution)/shard_map/while/body/eval_jaxpr/all_gather | solution.py:132
  15.5 130.6 %all-gather.20.cloned.1.call-start = ((), (), s32[]{:S(2)}) async-start(), calls=%async_computation.13 | async-start | bytes 3932160 | tf_op jit(solution)/shard_map/while/body/eval_jaxpr/all_gather | solution.py:152
  64.2 96.6 %all-gather.22.cloned.1.call-start = ((), (), s32[]{:S(2)}) async-start(), calls=%async_computation.14 | async-start | bytes 1474560 | tf_op jit(solution)/shard_map/while/body/eval_jaxpr/all_gather | solution.py:133
  64.9 101.1 %all-gather.24.cloned.1.call-start = ((), (), s32[]{:S(2)}) async-start(), calls=%async_computation.15 | async-start | bytes 4423680 | tf_op jit(solution)/shard_map/while/body/eval_jaxpr/all_gather | solution.py:134
  65.5 118.4 %all-gather.26.cloned.1.call-start = ((), (), s32[]{:S(2)}) async-start(), calls=%async_computation.16 | async-start | bytes 2211840 | tf_op jit(solution)/shard_map/while/body/eval_jaxpr/all_gather | solution.py:180
  70.4 34.6 %collective-permute-start.1 = (bf16[2,256,12,64]{1,3,2,0:T(8,128)(2,1)}, bf16[2,256,12,64]{1,3,2,0:T(8,128)(2,1)S(1)}, u32[]{:S(2)}, u32[]{:S(2)}) collective-permute-start(bf16[2,256,12,64]{1,3,2,0:T(8,128)(2,1)} %pad_maximum_fusion.9), channel_id=1, source_target_pairs={{0,1},{1,2},{2,3},{3,0},{4,5},{5,6},{6,7},{7,4},{8,9},{9,10},{10,1... | collective-permute-start | bytes 2359304 | tf_op jit(solution)/shard_map/while/body/eval_jaxpr/ppermute | solution.py:32
  70.6 222.1 %reduce-scatter.22.cloned.1.call-start = ((), (), s32[]{:S(2)}) async-start(), calls=%async_computation.18 | async-start | bytes 3932160 | tf_op jit(solution)/shard_map/while/body/eval_jaxpr/reduce_scatter | solution.py:232
  70.8 37.8 %collective-permute-start = (bf16[2,256,12,64]{1,3,2,0:T(8,128)(2,1)}, bf16[2,256,12,64]{1,3,2,0:T(8,128)(2,1)S(1)}, u32[]{:S(2)}, u32[]{:S(2)}) collective-permute-start(bf16[2,256,12,64]{1,3,2,0:T(8,128)(2,1)} %pad_maximum_fusion.9), channel_id=1, source_target_pairs={{1,0},{2,1},{3,2},{0,3},{5,4},{6,5},{7,6},{4,7},{9,8},{10,9},{11,1... | collective-permute-start | bytes 2359304 | tf_op jit(solution)/shard_map/while/body/eval_jaxpr/ppermute | solution.py:34
  248.1 78.8 %reduce-scatter.20.cloned.1.call-start = ((), (), s32[]{:S(2)}) async-start(), calls=%async_computation.17 | async-start | bytes 3932160 | tf_op jit(solution)/shard_map/while/body/eval_jaxpr/reduce_scatter | solution.py:235
  345.7 33.8 %all-gather.18.cloned.1.call-start = ((), (), s32[]{:S(2)}) async-start(), calls=%async_computation.12 | async-start | bytes 4423680 | tf_op jit(solution)/shard_map/while/body/eval_jaxpr/all_gather | solution.py:132
  346.6 128.0 %all-gather.20.cloned.1.call-start = ((), (), s32[]{:S(2)}) async-start(), calls=%async_computation.13 | async-start | bytes 3932160 | tf_op jit(solution)/shard_map/while/body/eval_jaxpr/all_gather | solution.py:152
  392.6 96.4 %all-gather.22.cloned.1.call-start = ((), (), s32[]{:S(2)}) async-start(), calls=%async_computation.14 | async-start | bytes 1474560 | tf_op jit(solution)/shard_map/while/body/eval_jaxpr/all_gather | solution.py:133
  393.1 101.1 %all-gather.24.cloned.1.call-start = ((), (), s32[]{:S(2)}) async-start(), calls=%async_computation.15 | async-start | bytes 4423680 | tf_op jit(solution)/shard_map/while/body/eval_jaxpr/all_gather | solution.py:134
  393.9 118.4 %all-gather.26.cloned.1.call-start = ((), (), s32[]{:S(2)}) async-start(), calls=%async_computation.16 | async-start | bytes 2211840 | tf_op jit(solution)/shard_map/while/body/eval_jaxpr/all_gather | solution.py:180
  398.8 34.6 %collective-permute-start.1 = (bf16[2,256,12,64]{1,3,2,0:T(8,128)(2,1)}, bf16[2,256,12,64]{1,3,2,0:T(8,128)(2,1)S(1)}, u32[]{:S(2)}, u32[]{:S(2)}) collective-permute-start(bf16[2,256,12,64]{1,3,2,0:T(8,128)(2,1)} %pad_maximum_fusion.9), channel_id=1, source_target_pairs={{0,1},{1,2},{2,3},{3,0},{4,5},{5,6},{6,7},{7,4},{8,9},{9,10},{10,1... | collective-permute-start | bytes 2359304 | tf_op jit(solution)/shard_map/while/body/eval_jaxpr/ppermute | solution.py:32
  399.0 226.3 %reduce-scatter.22.cloned.1.call-start = ((), (), s32[]{:S(2)}) async-start(), calls=%async_computation.18 | async-start | bytes 3932160 | tf_op jit(solution)/shard_map/while/body/eval_jaxpr/reduce_scatter | solution.py:232
  399.2 37.8 %collective-permute-start = (bf16[2,256,12,64]{1,3,2,0:T(8,128)(2,1)}, bf16[2,256,12,64]{1,3,2,0:T(8,128)(2,1)S(1)}, u32[]{:S(2)}, u32[]{:S(2)}) collective-permute-start(bf16[2,256,12,64]{1,3,2,0:T(8,128)(2,1)} %pad_maximum_fusion.9), channel_id=1, source_target_pairs={{1,0},{2,1},{3,2},{0,3},{5,4},{6,5},{7,6},{4,7},{9,8},{10,9},{11,1... | collective-permute-start | bytes 2359304 | tf_op jit(solution)/shard_map/while/body/eval_jaxpr/ppermute | solution.py:34
  433.4 11.4 %collective-permute-start.2 = (bf16[2,256,12,64]{1,3,2,0:T(8,128)(2,1)S(1)}, bf16[2,256,12,64]{1,3,2,0:T(8,128)(2,1)S(1)}, u32[]{:S(2)}, u32[]{:S(2)}) collective-permute-start(bf16[2,256,12,64]{1,3,2,0:T(8,128)(2,1)S(1)} %collective-permute-done.1), channel_id=1, source_target_pairs={{0,1},{1,2},{2,3},{3,0},{4,5},{5,6},{6,7},{7,4},{8,9},{9,10},{10,1... | collective-permute-start | bytes 2359304 | tf_op jit(solution)/shard_map/while/body/eval_jaxpr/ppermute | solution.py:32
  576.8 78.7 %reduce-scatter.20.cloned.1.call-start = ((), (), s32[]{:S(2)}) async-start(), calls=%async_computation.17 | async-start | bytes 3932160 | tf_op jit(solution)/shard_map/while/body/eval_jaxpr/reduce_scatter | solution.py:235
  678.9 23.2 %reduce-scatter.18.cloned.1.call-start = ((), (), s32[]{:S(2)}) async-start(), calls=%async_computation.11 | async-start | bytes 245760
  680.6 50.3 %reduce-scatter.12.cloned.1.call-start = ((), (), s32[]{:S(2)}) async-start(), calls=%async_computation.8 | async-start | bytes 1474560 | tf_op jit(solution)/shard_map/reduce_scatter | solution.py:269
  683.4 79.9 %reduce-scatter.16.cloned.1.call-start = ((), (), s32[]{:S(2)}) async-start(), calls=%async_computation.10 | async-start | bytes 2211840 | tf_op jit(solution)/shard_map/reduce_scatter | solution.py:275
  686.9 119.4 %reduce-scatter.10.cloned.1.call-start = ((), (), s32[]{:S(2)}) async-start(), calls=%async_computation.7 | async-start | bytes 4423680 | tf_op jit(solution)/shard_map/reduce_scatter | solution.py:266
  692.2 157.1 %reduce-scatter.14.cloned.1.call-start = ((), (), s32[]{:S(2)}) async-start(), calls=%async_computation.9 | async-start | bytes 4423680 | tf_op jit(solution)/shard_map/reduce_scatter | solution.py:272
  (154 other events, 2984.0 us)
Sparse Core Ops, SparseCore 0:
  17.6 33.4 all-gather.17
  64.3 44.9 all-gather.19
  110.9 17.3 all-gather.21
  130.3 30.7 all-gather.23
  163.1 20.7 all-gather.25
  248.2 37.9 reduce-scatter.21
  288.9 37.9 reduce-scatter.19
  348.6 30.7 all-gather.17
  392.7 44.9 all-gather.19
  439.1 17.4 all-gather.21
  458.7 30.7 all-gather.23
  491.5 20.7 all-gather.25
  576.9 37.9 reduce-scatter.21
  617.4 37.9 reduce-scatter.19
Sparse Core Ops, SparseCore 1:
  682.4 19.7 reduce-scatter.17
  705.2 25.6 reduce-scatter.11
  734.0 29.2 reduce-scatter.15
  765.9 40.3 reduce-scatter.9
  809.0 40.2 reduce-scatter.13
